TPU v7x, 256 devices: a whole 4x4x8 slice. The times are simulated.
256 devices in a mesh: tile: 128 (over y, x, z), dp: 2 (over core).
Axes of the slice: x: 4, y: 4, z: 8, core: 2. Of those that a mesh axis runs over, the one named last changes fastest.
Arguments:
- features: bfloat16 [2, 1536, 384, 128], P('dp', 'tile'), may hold values from -6 to 6
- cotangent: bfloat16 [2, 1536, 384, 128], P('dp', 'tile'), may hold values from -6 to 6
- tile_mask: int32 [2, 128, 32], P('dp', 'tile'), may hold values from 0 to 1, as said below
- work_lists: int32 [2, 128, 22], P('dp'), may hold values from 0 to 4095, as said below
- dilations: int32 [2, 128], P('dp'), may hold values from 1 to 2
- conv_weight: bfloat16 [3, 3, 128, 128], replicated, may hold values from -0.1875 to 0.1875
- conv_bias: float32 [128], replicated, may hold values from -4 to 4
Outputs:
- input_grad: bfloat16 [2, 1536, 384, 128], P('dp', 'tile')
- weight_grads: float32 [147456], P(('tile', 'dp'))
Inputs may be any that keep to these rules, and one draw needn't show every extreme that they name: `tile_mask`: exactly 2816 tiles of each copy are 1. `work_lists`: for each copy, the work lists name every tile whose mask is 1 exactly once, as row * 32 + column, 22 for each worker; at most 1 of one worker's ids lie in one row of tiles, and in every draw some worker has 1 ids in one row.
All inputs are finite; a program needn't handle non-finite values.
Results may differ from a plain program's by a relative error of at most 0.0055.
Values may be sent and summed in bfloat16 or wider, within the bound.
A program may use at most 128 MiB of HBM per device.

v0:
```python
import functools
import math

import jax
import jax.numpy as jnp
from jax import lax
from jax.experimental import pallas as pl
from jax.experimental.pallas import tpu as pltpu
from jax.sharding import Mesh
from jax.sharding import PartitionSpec as P

TILE = 12
HALO = 2
CH = 128
TAPS = 9
PAD = 8
TILE_AXES = ("tile_0", "tile_1", "tile_2")
TILE_DP = ("tile_0", "tile_1", "tile_2", "dp")
MESH = pl.DeviceIdType.MESH
F32 = jnp.float32
BF16 = jnp.bfloat16


def at(y, x, z, c):
    return {"tile_0": y, "tile_1": x, "tile_2": z, "dp": c}


def kernel(
    sizes,
    cells,
    dil_ref,
    mask_ref,
    bias_ref,
    w_ref,
    x_hbm,
    c_hbm,
    out_ref,
    wout_ref,
    xin,
    cin,
    mref,
    halo_out,
    halo_in,
    rim_out,
    rim_in,
    xf,
    x2,
    gf,
    g2,
    yf,
    rim2,
    wf,
    wi,
    acc,
    taps,
    core_in,
    half,
    plane_in,
    plane_sum,
    piece,
    piece_in,
    load_sem,
    halo_send,
    halo_recv,
    rim_send,
    rim_recv,
    core_send,
    core_recv,
    plane_send,
    plane_recv,
    z_send,
    z_recv,
):
    ny, nx, nz = sizes
    cols = x_hbm.shape[1]
    rows_total = TAPS * CH
    blocks = ny * nx
    block_rows = rows_total // blocks
    half_rows = half.shape[1]
    half_off = block_rows - half_rows
    chip_rows = block_rows // nz
    tiles_total = blocks * nz

    y = lax.axis_index("tile_0")
    x = lax.axis_index("tile_1")
    z = lax.axis_index("tile_2")
    c = lax.axis_index("dp")
    plane = y * nx + x
    r = plane * nz + z

    def row_device(row):
        row = lax.rem(row + tiles_total, tiles_total)
        return at(row // (nx * nz), (row // nz) % nx, row % nz, c)

    def plane_device(index):
        return at(index // nx, index % nx, z, c)

    load_x = pltpu.make_async_copy(x_hbm, xin, load_sem.at[0])
    load_c = pltpu.make_async_copy(c_hbm, cin, load_sem.at[1])
    load_x.start()
    load_c.start()

    barrier = pltpu.get_barrier_semaphore()
    pl.semaphore_signal(barrier, inc=1, device_id=row_device(r - 1), device_id_type=MESH)
    pl.semaphore_signal(barrier, inc=1, device_id=row_device(r + 1), device_id_type=MESH)
    pl.semaphore_signal(barrier, inc=1, device_id=at(y, x, z, 1 - c), device_id_type=MESH)
    for step in range(1, blocks):
        pl.semaphore_signal(
            barrier,
            inc=1,
            device_id=plane_device(lax.rem(plane + step, blocks)),
            device_id_type=MESH,
        )
    source_core = z // (nz // 2)
    for zz in range(nz):

        @pl.when(jnp.logical_not(jnp.logical_and(z == zz, c == source_core)))
        def _():
            pl.semaphore_signal(
                barrier, inc=1, device_id=at(y, x, zz, source_core), device_id_type=MESH
            )

    col = lax.broadcasted_iota(jnp.int32, (cols, cols // TILE), 0)
    tile = lax.broadcasted_iota(jnp.int32, (cols, cols // TILE), 1) * TILE
    inside = jnp.logical_and(col >= tile, col < tile + TILE)
    picked = jnp.where(inside, mask_ref[...].astype(F32), 0.0)
    column = jnp.sum(picked, axis=1, keepdims=True)
    mref[...] = jnp.broadcast_to(column, (cols, CH)).astype(BF16)

    d = dil_ref[0, r]
    d_up = dil_ref[0, lax.rem(r + tiles_total - 1, tiles_total)]
    d_down = dil_ref[0, lax.rem(r + 1, tiles_total)]

    load_x.wait()
    own = mref[...]
    halo_out[0] = xin[0:2] * own
    halo_out[1] = xin[10:12] * own
    extra = jnp.where(source_core == c, 1, 0)
    pl.semaphore_wait(barrier, 2 + 1 + (blocks - 1) + nz - extra)

    def halo_copy(side):
        return pltpu.make_async_remote_copy(
            src_ref=halo_out.at[side],
            dst_ref=halo_in.at[1 - side],
            send_sem=halo_send.at[side],
            recv_sem=halo_recv.at[1 - side],
            device_id=row_device(r - 1 if side == 0 else r + 1),
            device_id_type=MESH,
        )

    halo_copy(0).start()
    halo_copy(1).start()

    zero = jnp.zeros((CH, CH), BF16)
    for a in range(3):
        base = 2 * CH * a
        wf[base : base + CH, 0:CH] = w_ref[a, 1]
        wf[base : base + CH, CH:] = w_ref[a, 0]
        wf[base + CH : base + 2 * CH, 0:CH] = w_ref[a, 2]
        wf[base + CH : base + 2 * CH, CH:] = zero
        wi[base : base + CH, 0:CH] = w_ref[a, 1].T
        wi[base : base + CH, CH:] = w_ref[a, 2].T
        wi[base + CH : base + 2 * CH, 0:CH] = w_ref[a, 0].T
        wi[base + CH : base + 2 * CH, CH:] = zero

    margin_x = jnp.zeros((xf.shape[0], PAD, CH), F32)
    xf[:, cols:] = margin_x
    margin_g = jnp.zeros((2, PAD, CH), F32)
    gf[:, cols:] = margin_g
    yf[:, 0:PAD] = margin_g
    g2[0:2] = jnp.zeros((2, cols, 2 * CH), BF16)
    g2[14:16] = jnp.zeros((2, cols, 2 * CH), BF16)

    def put_x(row, value):
        xf[pl.ds(row, 2), 0:cols] = value.astype(F32)
        x2[pl.ds(row, 2), :, 0:CH] = value
        x2[pl.ds(row, 2), :, CH:] = xf[pl.ds(row, 2), pl.ds(d, cols)].astype(BF16)

    def own_rows(i, carry):
        put_x(2 + 2 * i, xin[pl.ds(2 * i, 2)] * mref[...])
        return carry

    lax.fori_loop(0, TILE // 2, own_rows, 0)
    load_c.wait()

    def stacked(ref, row, shift):
        parts = [
            ref[pl.ds(row - shift, 2)].reshape(2 * cols, 2 * CH),
            ref[pl.ds(row, 2)].reshape(2 * cols, 2 * CH),
            ref[pl.ds(row + shift, 2)].reshape(2 * cols, 2 * CH),
        ]
        return jnp.concatenate(parts, axis=1)

    def folded(product, shift):
        yf[:, PAD:] = product[:, CH:].reshape(2, cols, CH)
        return product[:, 0:CH].reshape(2, cols, CH) + yf[:, pl.ds(PAD - shift, cols)]

    def grad_rows(p):
        product = jnp.dot(stacked(x2, p + 2, d), wf[...], preferred_element_type=F32)
        pre = folded(product, d) + bias_ref[...]
        sig = jax.nn.sigmoid(pre)
        cot = (cin[pl.ds(p, 2)] * mref[...]).astype(F32)
        grad = (cot * sig * (1.0 + pre * (1.0 - sig))).astype(BF16)
        gf[:, 0:cols] = grad.astype(F32)
        g2[pl.ds(p + 2, 2), :, 0:CH] = grad
        g2[pl.ds(p + 2, 2), :, CH:] = gf[:, pl.ds(d, cols)].astype(BF16)
        return grad

    def inner_rows(i, carry):
        grad_rows(2 + 2 * i)
        return carry

    lax.fori_loop(0, 4, inner_rows, 0)

    acc[...] = jnp.zeros_like(acc)

    def tap_rows(p, a, turned):
        shifted = x2[pl.ds(p + 2 + (a - 1) * d, 2)].reshape(2 * cols, 2 * CH)
        return jnp.dot(turned, shifted, preferred_element_type=F32)

    def inner_taps(i, carry):
        p = 2 + 2 * i
        turned = g2[pl.ds(p + 2, 2)].reshape(2 * cols, 2 * CH).T
        for a in range(3):
            acc[a] += tap_rows(p, a, turned)
        return carry

    lax.fori_loop(0, 4, inner_taps, 0)

    halo_copy(0).wait()
    halo_copy(1).wait()
    above = halo_in[0]
    below = halo_in[1]
    put_x(0, jnp.where(r == 0, jnp.zeros_like(above), above))
    put_x(14, jnp.where(r == tiles_total - 1, jnp.zeros_like(below), below))
    rim_out[0] = grad_rows(0)
    rim_out[1] = grad_rows(10)

    def rim_copy(side):
        return pltpu.make_async_remote_copy(
            src_ref=rim_out.at[side],
            dst_ref=rim_in.at[1 - side],
            send_sem=rim_send.at[side],
            recv_sem=rim_recv.at[1 - side],
            device_id=row_device(r - 1 if side == 0 else r + 1),
            device_id_type=MESH,
        )

    rim_copy(0).start()
    rim_copy(1).start()

    groups = []
    first = 0
    for a in range(3):
        last = (3 * CH * (a + 1)) // block_rows
        groups.append((first, last - first))
        first = last

    def core_copy(index):
        start, count = groups[index]
        return pltpu.make_async_remote_copy(
            src_ref=taps.at[
                pl.ds(start, count), pl.ds(pl.multiple_of((1 - c) * half_off, 8), half_rows)
            ],
            dst_ref=core_in.at[pl.ds(start, count)],
            send_sem=core_send.at[index],
            recv_sem=core_recv.at[index],
            device_id=at(y, x, z, 1 - c),
            device_id_type=MESH,
        )

    turned_top = g2[2:4].reshape(2 * cols, 2 * CH).T
    turned_bottom = g2[12:14].reshape(2 * cols, 2 * CH).T
    for a in range(3):
        total = acc[a] + tap_rows(0, a, turned_top) + tap_rows(10, a, turned_bottom)
        parts = (total[CH:, 0:CH], total[0:CH, 0:CH], total[0:CH, CH:])
        for b in range(3):
            value = parts[b].T
            row = (3 * a + b) * CH
            done = 0
            while done < CH:
                block, offset = divmod(row + done, block_rows)
                size = min(CH - done, block_rows - offset)
                taps[block, offset : offset + size] = value[done : done + size]
                done += size
        core_copy(a).start()

    def input_rows(m, extra_rows=None):
        product = jnp.dot(
            stacked(g2, m + 2, -d), wi[...], preferred_element_type=F32
        )
        value = folded(product, d)
        own_mask = mref[...].astype(F32)
        value = value + cin[pl.ds(m, 2)].astype(F32)
        if extra_rows is not None:
            value = value + extra_rows
        out_ref[pl.ds(m, 2)] = (value * own_mask).astype(BF16)

    def plane_copy(step):
        target = lax.rem(plane + step, blocks)
        return pltpu.make_async_remote_copy(
            src_ref=half.at[target],
            dst_ref=plane_in.at[plane],
            send_sem=plane_send.at[step],
            recv_sem=plane_recv.at[step],
            device_id=plane_device(target),
            device_id_type=MESH,
        )

    def plane_arrival(step):
        source = lax.rem(plane + blocks - step, blocks)
        return pltpu.make_async_remote_copy(
            src_ref=half.at[source],
            dst_ref=plane_in.at[source],
            send_sem=plane_send.at[step],
            recv_sem=plane_recv.at[step],
            device_id=plane_device(source),
            device_id_type=MESH,
        )

    for index in range(3):
        core_copy(index).wait()
        start, count = groups[index]
        mine = taps[pl.ds(start, count), pl.ds(pl.multiple_of(c * half_off, 8), half_rows)]
        half[start : start + count] = mine + core_in[start : start + count]
    for step in range(1, blocks):
        plane_copy(step).start()

    def inner_input(i, carry):
        input_rows(2 + 2 * i)
        return carry

    lax.fori_loop(0, 4, inner_input, 0)

    total = half[plane]
    for step in range(1, blocks):
        plane_arrival(step).wait_recv()
        total = total + plane_in[lax.rem(plane + blocks - step, blocks)]
    plane_sum[...] = total
    near = nz // 2

    def z_copy(k, core):
        return pltpu.make_async_remote_copy(
            src_ref=piece.at[k],
            dst_ref=piece_in.at[z],
            send_sem=z_send.at[2 * k + core],
            recv_sem=z_recv.at[z],
            device_id=at(y, x, near * c + k, core),
            device_id_type=MESH,
        )

    def is_self(k, core):
        return jnp.logical_and(near * c + k == z, c == core)

    for k in range(near):
        offset = chip_rows * k + c * (chip_rows * near - half_off)
        piece[k] = plane_sum[pl.ds(offset, chip_rows)]
    for k in range(near):
        for core in range(2):

            @pl.when(jnp.logical_not(is_self(k, core)))
            def _():
                z_copy(k, core).start()

            @pl.when(is_self(k, core))
            def _():
                piece_in[z] = piece[k]

    rim_copy(0).wait()
    rim_copy(1).wait()

    def rim_rows(side, rate, edge):
        got = rim_in[side]
        nothing = jnp.zeros_like(got[0:1])
        wide = rate == 2
        if side == 0:
            rows = jnp.concatenate(
                [jnp.where(wide, got[0:1], got[1:2]), jnp.where(wide, got[1:2], nothing)], axis=0
            )
            weight = wi[4 * CH : 6 * CH]
        else:
            rows = jnp.concatenate(
                [jnp.where(wide, got[0:1], nothing), jnp.where(wide, got[1:2], got[0:1])], axis=0
            )
            weight = wi[0 : 2 * CH]
        rows = jnp.where(edge, jnp.zeros_like(rows), rows)
        gf[:, 0:cols] = rows.astype(F32)
        rim2[:, :, 0:CH] = rows
        rim2[:, :, CH:] = gf[:, pl.ds(rate, cols)].astype(BF16)
        product = jnp.dot(
            rim2[...].reshape(2 * cols, 2 * CH), weight, preferred_element_type=F32
        )
        return folded(product, rate)

    input_rows(0, rim_rows(0, d_up, r == 0))
    input_rows(10, rim_rows(1, d_down, r == tiles_total - 1))

    for step in range(1, blocks):
        plane_copy(step).wait_send()
    for k in range(near):
        for core in range(2):

            @pl.when(jnp.logical_not(is_self(k, core)))
            def _():
                z_copy(k, core).wait_send()

    for zz in range(nz):

        @pl.when(jnp.logical_not(jnp.logical_and(z == zz, c == source_core)))
        def _():
            pltpu.make_async_remote_copy(
                src_ref=piece.at[0],
                dst_ref=piece_in.at[zz],
                send_sem=z_send.at[0],
                recv_sem=z_recv.at[zz],
                device_id=at(y, x, zz, source_core),
                device_id_type=MESH,
            ).wait_recv()

    final = piece_in[0]
    for zz in range(1, nz):
        final = final + piece_in[zz]
    scale = 1.0 / math.sqrt(cells)
    wout_ref[...] = final * scale


def shards(sizes, features, cotangent, tile_mask, work_lists, dilations, conv_weight, conv_bias):
    ny, nx, nz = sizes
    own_strip = features[0]
    own_cotan = cotangent[0]
    cols = own_strip.shape[1]
    blocks = ny * nx
    block_rows = TAPS * CH // blocks
    half_rows = -(-(block_rows // 2) // 8) * 8
    chip_rows = block_rows // nz
    cells = blocks * nz * 2 * work_lists.shape[2] * TILE * TILE
    vmem = pl.BlockSpec(memory_space=pltpu.VMEM)
    hbm = pl.BlockSpec(memory_space=pl.ANY)
    dma = pltpu.SemaphoreType.DMA
    input_grad, chip_grad = pl.pallas_call(
        functools.partial(kernel, sizes, cells),
        out_shape=(
            jax.ShapeDtypeStruct(own_strip.shape, BF16),
            jax.ShapeDtypeStruct((chip_rows, CH), F32),
        ),
        in_specs=[pl.BlockSpec(memory_space=pltpu.SMEM), vmem, vmem, vmem, hbm, hbm],
        out_specs=(vmem, vmem),
        scratch_shapes=[
            pltpu.VMEM((TILE, cols, CH), BF16),
            pltpu.VMEM((TILE, cols, CH), BF16),
            pltpu.VMEM((cols, CH), BF16),
            pltpu.VMEM((2, HALO, cols, CH), BF16),
            pltpu.VMEM((2, HALO, cols, CH), BF16),
            pltpu.VMEM((2, HALO, cols, CH), BF16),
            pltpu.VMEM((2, HALO, cols, CH), BF16),
            pltpu.VMEM((16, cols + PAD, CH), F32),
            pltpu.VMEM((16, cols, 2 * CH), BF16),
            pltpu.VMEM((2, cols + PAD, CH), F32),
            pltpu.VMEM((16, cols, 2 * CH), BF16),
            pltpu.VMEM((2, cols + PAD, CH), F32),
            pltpu.VMEM((2, cols, 2 * CH), BF16),
            pltpu.VMEM((6 * CH, 2 * CH), BF16),
            pltpu.VMEM((6 * CH, 2 * CH), BF16),
            pltpu.VMEM((3, 2 * CH, 2 * CH), F32),
            pltpu.VMEM((blocks, block_rows, CH), F32),
            pltpu.VMEM((blocks, half_rows, CH), F32),
            pltpu.VMEM((blocks, half_rows, CH), F32),
            pltpu.VMEM((blocks, half_rows, CH), F32),
            pltpu.VMEM((half_rows, CH), F32),
            pltpu.VMEM((nz // 2, chip_rows, CH), F32),
            pltpu.VMEM((nz, chip_rows, CH), F32),
            dma((2,)),
            dma((2,)),
            dma((2,)),
            dma((2,)),
            dma((2,)),
            dma((3,)),
            dma((3,)),
            dma((blocks,)),
            dma((blocks,)),
            dma((nz,)),
            dma((nz,)),
        ],
        compiler_params=pltpu.CompilerParams(
            collective_id=0, has_side_effects=True, vmem_limit_bytes=56 * 1024 * 1024
        ),
    )(
        dilations,
        tile_mask.reshape(1, -1),
        conv_bias.reshape(1, -1),
        conv_weight,
        own_strip,
        own_cotan,
    )
    weight_grads = lax.dynamic_index_in_dim(
        chip_grad.reshape(2, -1), lax.axis_index("dp"), axis=0, keepdims=False
    )
    return (input_grad[None], weight_grads)


def torus_sizes(devices):
    return (4, 4, devices // 16)


def solution(mesh):
    ny, nx, nz = torus_sizes(mesh.shape["tile"])
    torus = Mesh(mesh.devices.reshape(ny, nx, nz, mesh.shape["dp"]), TILE_DP)
    in_specs = (
        P("dp", TILE_AXES, None, None),
        P("dp", TILE_AXES, None, None),
        P("dp", TILE_AXES, None),
        P("dp", None, None),
        P("dp", None),
        P(),
        P(),
    )
    out_specs = (P("dp", TILE_AXES, None, None), P(TILE_DP))
    return jax.shard_map(
        functools.partial(shards, (ny, nx, nz)),
        mesh=torus,
        in_specs=in_specs,
        out_specs=out_specs,
        check_vma=False,
    )
```

profile of v0, /device:TPU:1, one launch (start us, length us, event | category | flops | bytes accessed | tf_op | source)
XLA Modules:
  0.0 41.8 jit_solution(18339093284726022635)
XLA Ops:
  0.6 37.5 %shard_map.77 = (bf16[12,384,128]{2,1,0:T(8,128)(2,1)}, f32[9,128]{1,0:T(8,128)}) custom-call(s32[1,128]{1,0:T(1,128)} %dil_ref.1, s32[1,32]{1,0:T(1,128)} %bitcast.8, f32[1,128]{1,0:T(1,128)} %bitcast.9, bf16[3,3,128,128]{3,2,1,0:T(8,128)(2,1)} %w_ref.1, bf16[12,384,128]{2,1,0:T(8,128)(2,1)} %bitcast.5, bf16[12,384,128]{2,1,0:T(8,128)(2,1)} %bitcast.6), custom_call_target="tpu_custom_call" | custom-call | tf_op jit(solution)/shard_map/pallas_call | solution.py:440
  38.1 0.8 %reshape.15 = f32[2,576]{1,0:T(2,128)S(1)} reshape(f32[9,128]{1,0:T(8,128)} %get-tuple-element.5) | data formatting | bytes 9216 | tf_op jit(solution)/shard_map/reshape | solution.py:496
  38.9 0.6 %dynamic-slice_reduce_fusion = f32[576]{0:T(1024)} fusion(f32[2,576]{1,0:T(2,128)S(1)} %reshape.15, s32[]{:T(128)S(6)} %select_n.4), kind=kLoop, calls=%fused_computation | loop fusion | bytes 4612 | tf_op jit(solution)/shard_map/jit(dynamic_index_in_dim)/dynamic_slice | solution.py:495
  39.5 2.4 %copy.9 = bf16[1,12,384,128]{3,2,1,0:T(8,128)(2,1)} copy(bf16[1,12,384,128]{3,2,1,0:T(8,128)(2,1)} %bitcast.7) | data formatting | bytes 2359296
where the time goes:
time: 42.1 us; the launch traced here: 41.8 us
  Pallas kernels  37.5 us (89%)
  local copies, waits for them, and re-layouts  3.74 us (9%)
  between operations  0.64 us (2%)
    pallas_call x1, Pallas kernels, shards(): pl.pallas_call(functools.partial(kernel, sizes, cells), out_shape=(jax.Sh...  37.5 us
    unnamed x1, local copies, waits for them, and re-layouts  2.36 us

commit v1 on v0

--- a/solution.py
+++ b/solution.py
@@ -28,14 +28,18 @@
 def kernel(
     sizes,
     cells,
+    dil_hbm,
+    mask_hbm,
+    bias_hbm,
+    w_hbm,
+    x_hbm,
+    c_hbm,
+    out_ref,
+    wout_ref,
     dil_ref,
     mask_ref,
     bias_ref,
     w_ref,
-    x_hbm,
-    c_hbm,
-    out_ref,
-    wout_ref,
     xin,
     cin,
     mref,
@@ -97,7 +101,15 @@
 
     load_x = pltpu.make_async_copy(x_hbm, xin, load_sem.at[0])
     load_c = pltpu.make_async_copy(c_hbm, cin, load_sem.at[1])
+    load_w = pltpu.make_async_copy(w_hbm, w_ref, load_sem.at[2])
+    load_dil = pltpu.make_async_copy(dil_hbm, dil_ref, load_sem.at[3])
+    load_mask = pltpu.make_async_copy(mask_hbm, mask_ref, load_sem.at[4])
+    load_bias = pltpu.make_async_copy(bias_hbm, bias_ref, load_sem.at[5])
+    load_mask.start()
+    load_dil.start()
     load_x.start()
+    load_bias.start()
+    load_w.start()
     load_c.start()
 
     barrier = pltpu.get_barrier_semaphore()
@@ -123,10 +135,13 @@
     col = lax.broadcasted_iota(jnp.int32, (cols, cols // TILE), 0)
     tile = lax.broadcasted_iota(jnp.int32, (cols, cols // TILE), 1) * TILE
     inside = jnp.logical_and(col >= tile, col < tile + TILE)
+    load_mask.wait()
     picked = jnp.where(inside, mask_ref[...].astype(F32), 0.0)
     column = jnp.sum(picked, axis=1, keepdims=True)
     mref[...] = jnp.broadcast_to(column, (cols, CH)).astype(BF16)
 
+    load_dil.wait()
+    load_bias.wait()
     d = dil_ref[0, r]
     d_up = dil_ref[0, lax.rem(r + tiles_total - 1, tiles_total)]
     d_down = dil_ref[0, lax.rem(r + 1, tiles_total)]
@@ -135,22 +150,7 @@
     own = mref[...]
     halo_out[0] = xin[0:2] * own
     halo_out[1] = xin[10:12] * own
-    extra = jnp.where(source_core == c, 1, 0)
-    pl.semaphore_wait(barrier, 2 + 1 + (blocks - 1) + nz - extra)
-
-    def halo_copy(side):
-        return pltpu.make_async_remote_copy(
-            src_ref=halo_out.at[side],
-            dst_ref=halo_in.at[1 - side],
-            send_sem=halo_send.at[side],
-            recv_sem=halo_recv.at[1 - side],
-            device_id=row_device(r - 1 if side == 0 else r + 1),
-            device_id_type=MESH,
-        )
-
-    halo_copy(0).start()
-    halo_copy(1).start()
-
+    load_w.wait()
     zero = jnp.zeros((CH, CH), BF16)
     for a in range(3):
         base = 2 * CH * a
@@ -181,6 +181,23 @@
         return carry
 
     lax.fori_loop(0, TILE // 2, own_rows, 0)
+
+    extra = jnp.where(source_core == c, 1, 0)
+    pl.semaphore_wait(barrier, 2 + 1 + (blocks - 1) + nz - extra)
+
+    def halo_copy(side):
+        return pltpu.make_async_remote_copy(
+            src_ref=halo_out.at[side],
+            dst_ref=halo_in.at[1 - side],
+            send_sem=halo_send.at[side],
+            recv_sem=halo_recv.at[1 - side],
+            device_id=row_device(r - 1 if side == 0 else r + 1),
+            device_id_type=MESH,
+        )
+
+    halo_copy(0).start()
+    halo_copy(1).start()
+
     load_c.wait()
 
     def stacked(ref, row, shift):
@@ -420,8 +437,20 @@
     final = piece_in[0]
     for zz in range(1, nz):
         final = final + piece_in[zz]
-    scale = 1.0 / math.sqrt(cells)
-    wout_ref[...] = final * scale
+    final = final * (1.0 / math.sqrt(cells))
+    wide, rest = divmod(chip_rows, 2)
+    if rest == 0:
+        wout_ref[...] = jnp.where(c == 0, final[:wide], final[wide:])
+    else:
+        lane = lax.broadcasted_iota(jnp.int32, (1, CH), 1)
+        turned = jnp.concatenate([final[:, CH // 2 :], final[:, : CH // 2]], axis=1)
+        for k in range(wide):
+            low = wide + k
+            upper = jnp.where(lane < CH // 2, turned[low : low + 1], turned[low + 1 : low + 2])
+            value = jnp.where(c == 0, final[k : k + 1], upper)
+            wout_ref[k * CH : (k + 1) * CH] = value.reshape(CH)
+        last = jnp.where(c == 0, final[wide : wide + 1], turned[chip_rows - 1 :])
+        wout_ref[wide * CH :] = last.reshape(CH)[: CH // 2]
 
 
 def shards(sizes, features, cotangent, tile_mask, work_lists, dilations, conv_weight, conv_bias):
@@ -434,18 +463,32 @@
     half_rows = -(-(block_rows // 2) // 8) * 8
     chip_rows = block_rows // nz
     cells = blocks * nz * 2 * work_lists.shape[2] * TILE * TILE
+    odd = chip_rows % 2
+    grad_shape = (chip_rows * CH // 2,) if odd else (chip_rows // 2, CH)
     vmem = pl.BlockSpec(memory_space=pltpu.VMEM)
-    hbm = pl.BlockSpec(memory_space=pl.ANY)
+    hbm = pl.BlockSpec(memory_space=pltpu.HBM)
     dma = pltpu.SemaphoreType.DMA
+    operands = (
+        dilations,
+        tile_mask.reshape(1, -1),
+        conv_bias.reshape(1, -1),
+        conv_weight,
+        own_strip,
+        own_cotan,
+    )
     input_grad, chip_grad = pl.pallas_call(
         functools.partial(kernel, sizes, cells),
         out_shape=(
             jax.ShapeDtypeStruct(own_strip.shape, BF16),
-            jax.ShapeDtypeStruct((chip_rows, CH), F32),
+            jax.ShapeDtypeStruct(grad_shape, F32),
         ),
-        in_specs=[pl.BlockSpec(memory_space=pltpu.SMEM), vmem, vmem, vmem, hbm, hbm],
+        in_specs=[hbm] * 6,
         out_specs=(vmem, vmem),
         scratch_shapes=[
+            pltpu.SMEM(dilations.shape, jnp.int32),
+            pltpu.VMEM((1, cols // TILE), jnp.int32),
+            pltpu.VMEM((1, CH), F32),
+            pltpu.VMEM(conv_weight.shape, BF16),
             pltpu.VMEM((TILE, cols, CH), BF16),
             pltpu.VMEM((TILE, cols, CH), BF16),
             pltpu.VMEM((cols, CH), BF16),
@@ -469,7 +512,7 @@
             pltpu.VMEM((half_rows, CH), F32),
             pltpu.VMEM((nz // 2, chip_rows, CH), F32),
             pltpu.VMEM((nz, chip_rows, CH), F32),
-            dma((2,)),
+            dma((6,)),
             dma((2,)),
             dma((2,)),
             dma((2,)),
@@ -482,20 +525,10 @@
             dma((nz,)),
         ],
         compiler_params=pltpu.CompilerParams(
-            collective_id=0, has_side_effects=True, vmem_limit_bytes=56 * 1024 * 1024
+            collective_id=0, has_side_effects=True, vmem_limit_bytes=28 * 1024 * 1024
         ),
-    )(
-        dilations,
-        tile_mask.reshape(1, -1),
-        conv_bias.reshape(1, -1),
-        conv_weight,
-        own_strip,
-        own_cotan,
-    )
-    weight_grads = lax.dynamic_index_in_dim(
-        chip_grad.reshape(2, -1), lax.axis_index("dp"), axis=0, keepdims=False
-    )
-    return (input_grad[None], weight_grads)
+    )(*[pltpu.with_memory_space_constraint(value, pltpu.HBM) for value in operands])
+    return (input_grad[None], chip_grad.reshape(-1))
 
 
 def torus_sizes(devices):

time: 42.1 us -> 37.9 us (0.900)
  local copies, waits for them, and re-layouts: 3.74 us -> 1.61 us
  Pallas kernels: 37.5 us -> 35.6 us
    pallas_call x1, Pallas kernels: 37.5 us -> 35.6 us  [shards(): pl.pallas_call(functools.partial(kernel, sizes, cells), out_shape=(jax.Sh...]
    reshape x1 -> x0, local copies, waits for them, and re-layouts: 0.78 us -> none  [shards(): chip_grad.reshape(2, -1)]
    unnamed x1 -> x2, local copies, waits for them, and re-layouts: 2.36 us -> 1.61 us
    dynamic_slice x1 -> x0, local copies, waits for them, and re-layouts: 0.61 us -> none  [shards(): lax.dynamic_index_in_dim(chip_grad.reshape(2, -1), lax.axis_index('dp'),...]
where the time goes in v1:
time: 37.9 us; the launch traced here: 37.8 us
  Pallas kernels  35.6 us (94%)
  local copies, waits for them, and re-layouts  1.61 us (4%)
  between operations  0.64 us (2%)
    pallas_call x1, Pallas kernels, shards(): pl.pallas_call(functools.partial(kernel, sizes, cells), out_shape=(jax.Sh...  35.6 us
    unnamed x2, local copies, waits for them, and re-layouts  1.61 us

profile of v1, /device:TPU:1, one launch (start us, length us, event | category | flops | bytes accessed | tf_op | source)
XLA Modules:
  0.0 37.8 jit_solution(1550405198712163049)
XLA Ops:
  0.6 35.6 %shard_map.77 = (bf16[12,384,128]{2,1,0:T(8,128)(2,1)S(1)}, f32[576]{0:T(1024)S(1)}) custom-call(s32[1,128]{1,0:T(1,128)} %dil_hbm.1, s32[1,32]{1,0:T(1,128)} %bitcast.8, f32[1,128]{1,0:T(1,128)} %bitcast.9, bf16[3,3,128,128]{3,2,1,0:T(8,128)(2,1)} %w_hbm.1, bf16[12,384,128]{2,1,0:T(8,128)(2,1)} %bitcast.6, bf16[12,384,128]{2,1,0:T(8,128)(2,1)} %bitcast.7), custom_call_target="tpu_custom_call" | custom-call | tf_op jit(solution)/shard_map/pallas_call | solution.py:479
  36.2 1.0 %copy.10 = bf16[1,12,384,128]{3,2,1,0:T(8,128)(2,1)} copy(bf16[1,12,384,128]{3,2,1,0:T(8,128)(2,1)S(1)} %bitcast.5) | data formatting | bytes 2359296
  37.2 0.6 %copy.11 = f32[576]{0:T(1024)} copy(f32[576]{0:T(1024)S(1)} %get-tuple-element.9) | data formatting | bytes 4608

commit v2 on v1

v2 whole, which is shorter than its diff:
```python
import functools
import math

import jax
import jax.numpy as jnp
from jax import lax
from jax.experimental import pallas as pl
from jax.experimental.pallas import tpu as pltpu
from jax.sharding import Mesh
from jax.sharding import PartitionSpec as P

TILE = 12
HALO = 2
CH = 128
TAPS = 9
PAD = 8
TILE_AXES = ("tile_0", "tile_1", "tile_2")
TILE_DP = ("tile_0", "tile_1", "tile_2", "dp")
MESH = pl.DeviceIdType.MESH
F32 = jnp.float32
BF16 = jnp.bfloat16


def at(y, x, z, c):
    return {"tile_0": y, "tile_1": x, "tile_2": z, "dp": c}


def kernel(
    sizes,
    cells,
    dil_hbm,
    mask_hbm,
    bias_hbm,
    w_hbm,
    x_hbm,
    c_hbm,
    out_ref,
    wout_ref,
    dil_ref,
    mask_ref,
    bias_ref,
    w_ref,
    xin,
    cin,
    mref,
    halo_out,
    halo_in,
    rim_out,
    rim_in,
    xf,
    x2,
    gf,
    g2,
    yf,
    rim2,
    xh,
    pr,
    wf,
    wi,
    acc,
    taps,
    plane_in,
    plane_sum,
    piece,
    piece_in,
    load_sem,
    halo_send,
    halo_recv,
    rim_send,
    rim_recv,
    plane_send,
    plane_recv,
    z_send,
    z_recv,
):
    ny, nx, nz = sizes
    cols = x_hbm.shape[1]
    rows_total = TAPS * CH
    blocks = ny * nx
    block_rows = rows_total // blocks
    core_rows = piece.shape[1]
    chip_rows = block_rows // nz
    tiles_total = blocks * nz

    y = lax.axis_index("tile_0")
    x = lax.axis_index("tile_1")
    z = lax.axis_index("tile_2")
    c = lax.axis_index("dp")
    plane = y * nx + x
    r = plane * nz + z

    def row_device(row):
        row = lax.rem(row + tiles_total, tiles_total)
        return at(row // (nx * nz), (row // nz) % nx, row % nz, c)

    def plane_device(index):
        return at(index // nx, index % nx, z, c)

    column = 2 * z + c

    def column_device(index):
        return at(y, x, index // 2, index % 2)

    load_x = pltpu.make_async_copy(x_hbm, xin, load_sem.at[0])
    load_c = pltpu.make_async_copy(c_hbm, cin, load_sem.at[1])
    load_w = pltpu.make_async_copy(w_hbm, w_ref, load_sem.at[2])
    load_dil = pltpu.make_async_copy(dil_hbm, dil_ref, load_sem.at[3])
    load_mask = pltpu.make_async_copy(mask_hbm, mask_ref, load_sem.at[4])
    load_bias = pltpu.make_async_copy(bias_hbm, bias_ref, load_sem.at[5])
    load_mask.start()
    load_dil.start()
    load_x.start()
    load_bias.start()
    load_w.start()
    load_c.start()

    barrier = pltpu.get_barrier_semaphore()
    pl.semaphore_signal(barrier, inc=1, device_id=row_device(r - 1), device_id_type=MESH)
    pl.semaphore_signal(barrier, inc=1, device_id=row_device(r + 1), device_id_type=MESH)
    for step in range(1, blocks):
        pl.semaphore_signal(
            barrier,
            inc=1,
            device_id=plane_device(lax.rem(plane + step, blocks)),
            device_id_type=MESH,
        )
    for step in range(1, 2 * nz):
        pl.semaphore_signal(
            barrier,
            inc=1,
            device_id=column_device(lax.rem(column + step, 2 * nz)),
            device_id_type=MESH,
        )

    col = lax.broadcasted_iota(jnp.int32, (cols, cols // TILE), 0)
    tile = lax.broadcasted_iota(jnp.int32, (cols, cols // TILE), 1) * TILE
    inside = jnp.logical_and(col >= tile, col < tile + TILE)
    load_mask.wait()
    picked = jnp.where(inside, mask_ref[...].astype(F32), 0.0)
    observed = jnp.sum(picked, axis=1, keepdims=True)
    mref[...] = jnp.broadcast_to(observed, (cols, CH)).astype(BF16)

    load_dil.wait()
    load_bias.wait()
    d = dil_ref[0, r]
    d_up = dil_ref[0, lax.rem(r + tiles_total - 1, tiles_total)]
    d_down = dil_ref[0, lax.rem(r + 1, tiles_total)]

    load_x.wait()
    own = mref[...]
    halo_out[0] = xin[0:2] * own
    halo_out[1] = xin[10:12] * own
    load_w.wait()
    zero = jnp.zeros((CH, CH), BF16)
    for a in range(3):
        base = 2 * CH * a
        wf[base : base + CH, 0:CH] = w_ref[a, 1]
        wf[base : base + CH, CH:] = w_ref[a, 0]
        wf[base + CH : base + 2 * CH, 0:CH] = w_ref[a, 2]
        wf[base + CH : base + 2 * CH, CH:] = zero
        wi[base : base + CH, 0:CH] = w_ref[a, 1].T
        wi[base : base + CH, CH:] = w_ref[a, 2].T
        wi[base + CH : base + 2 * CH, 0:CH] = w_ref[a, 0].T
        wi[base + CH : base + 2 * CH, CH:] = zero

    margin_x = jnp.zeros((xf.shape[0], PAD, CH), F32)
    xf[:, cols:] = margin_x
    margin_g = jnp.zeros((2, PAD, CH), F32)
    gf[:, cols:] = margin_g
    yf[:, 0:PAD] = margin_g
    g2[0:2] = jnp.zeros((2, cols, 2 * CH), BF16)
    g2[14:16] = jnp.zeros((2, cols, 2 * CH), BF16)
    x2[0:2] = jnp.zeros((2, cols, 2 * CH), BF16)
    x2[14:16] = jnp.zeros((2, cols, 2 * CH), BF16)
    xh[0, 2:4] = jnp.zeros((2, cols, 2 * CH), BF16)
    xh[1, 0:2] = jnp.zeros((2, cols, 2 * CH), BF16)

    def put_x(row, value):
        xf[pl.ds(row, 2), 0:cols] = value.astype(F32)
        x2[pl.ds(row, 2), :, 0:CH] = value
        x2[pl.ds(row, 2), :, CH:] = xf[pl.ds(row, 2), pl.ds(d, cols)].astype(BF16)

    def own_rows(i, carry):
        put_x(2 + 2 * i, xin[pl.ds(2 * i, 2)] * mref[...])
        return carry

    lax.fori_loop(0, TILE // 2, own_rows, 0)

    pl.semaphore_wait(barrier, 2 + (blocks - 1) + (2 * nz - 1))

    def row_copy(sent, got, send, recv, side, k):
        return pltpu.make_async_remote_copy(
            src_ref=sent.at[side, k],
            dst_ref=got.at[1 - side, k],
            send_sem=send.at[side, k],
            recv_sem=recv.at[1 - side, k],
            device_id=row_device(r - 1 if side == 0 else r + 1),
            device_id_type=MESH,
        )

    def halo_copy(side, k):
        return row_copy(halo_out, halo_in, halo_send, halo_recv, side, k)

    def rim_copy(side, k):
        return row_copy(rim_out, rim_in, rim_send, rim_recv, side, k)

    halo_copy(0, 0).start()
    halo_copy(1, 1).start()
    halo_copy(0, 1).start()
    halo_copy(1, 0).start()

    load_c.wait()

    def stacked(ref, row, shift):
        parts = [
            ref[pl.ds(row - shift, 2)].reshape(2 * cols, 2 * CH),
            ref[pl.ds(row, 2)].reshape(2 * cols, 2 * CH),
            ref[pl.ds(row + shift, 2)].reshape(2 * cols, 2 * CH),
        ]
        return jnp.concatenate(parts, axis=1)

    def folded(product, shift, n):
        yf[0:n, PAD:] = product[:, CH:].reshape(n, cols, CH)
        return product[:, 0:CH].reshape(n, cols, CH) + yf[0:n, pl.ds(PAD - shift, cols)]

    def grad_rows(product, p, n):
        pre = folded(product, d, n) + bias_ref[...]
        turn = 0.5 * jnp.tanh(0.5 * pre)
        cot = (cin[pl.ds(p, n)] * mref[...]).astype(F32)
        grad = (cot * (0.5 + turn) * (1.0 + pre * (0.5 - turn))).astype(BF16)
        gf[0:n, 0:cols] = grad.astype(F32)
        g2[pl.ds(p + 2, n), :, 0:CH] = grad
        g2[pl.ds(p + 2, n), :, CH:] = gf[0:n, pl.ds(d, cols)].astype(BF16)
        return grad

    def inner_rows(i, carry):
        p = 2 + 2 * i
        product = jnp.dot(stacked(x2, p + 2, d), wf[...], preferred_element_type=F32)
        grad_rows(product, p, 2)
        return carry

    lax.fori_loop(0, 4, inner_rows, 0)

    for side in range(2):
        product = jnp.dot(
            stacked(x2, 2 + 10 * side, d), wf[...], preferred_element_type=F32
        )
        pr[side] = product.reshape(2, cols, 2 * CH)

    acc[...] = jnp.zeros_like(acc)

    def tap_rows(p, a, turned):
        shifted = x2[pl.ds(p + 2 + (a - 1) * d, 2)].reshape(2 * cols, 2 * CH)
        return jnp.dot(turned, shifted, preferred_element_type=F32)

    def inner_taps(i, carry):
        p = 2 + 2 * i
        turned = g2[pl.ds(p + 2, 2)].reshape(2 * cols, 2 * CH).T
        for a in range(3):
            acc[a] += tap_rows(p, a, turned)
        return carry

    lax.fori_loop(0, 4, inner_taps, 0)

    def put_halo(side, k):
        got = halo_in[side, k]
        edge = r == (0 if side == 0 else tiles_total - 1)
        value = jnp.where(edge, jnp.zeros_like(got), got)
        row = 14 * side + k
        xf[row, 0:cols] = value.astype(F32)
        moved = xf[row, pl.ds(d, cols)].astype(BF16)
        x2[row, :, 0:CH] = value
        x2[row, :, CH:] = moved
        xh[side, 2 * side + k, :, 0:CH] = value
        xh[side, 2 * side + k, :, CH:] = moved

    def rim_row(side, k):
        at_row = k + 2 - d if side == 0 else k + d
        weight = wf[4 * CH * side : 4 * CH * side + 2 * CH]
        product = pr[side, k] + jnp.dot(
            xh[side, at_row], weight, preferred_element_type=F32
        )
        rim_out[side, k] = grad_rows(product, 10 * side + k, 1)[0]

    def halo_wait(side, k):
        halo_copy(1 - side, k).wait_recv()

    halo_wait(0, 1)
    halo_wait(1, 0)
    put_halo(0, 1)
    put_halo(1, 0)
    rim_row(0, 1)
    rim_row(1, 0)
    rim_copy(0, 1).start()
    rim_copy(1, 0).start()
    halo_wait(0, 0)
    halo_wait(1, 1)
    put_halo(0, 0)
    put_halo(1, 1)
    rim_row(0, 0)
    rim_row(1, 1)
    rim_copy(0, 0).start()
    rim_copy(1, 1).start()

    groups = []
    first = 0
    for a in range(3):
        last = (3 * CH * (a + 1)) // block_rows
        groups.append((first, last))
        first = last

    def plane_copy(block):
        return pltpu.make_async_remote_copy(
            src_ref=taps.at[block],
            dst_ref=plane_in.at[plane],
            send_sem=plane_send.at[block],
            recv_sem=plane_recv.at[plane],
            device_id=plane_device(block),
            device_id_type=MESH,
        )

    def plane_arrival(source):
        return pltpu.make_async_remote_copy(
            src_ref=taps.at[source],
            dst_ref=plane_in.at[source],
            send_sem=plane_send.at[source],
            recv_sem=plane_recv.at[source],
            device_id=plane_device(source),
            device_id_type=MESH,
        )

    def others(count, own, action):
        for index in range(count[0], count[1]):

            @pl.when(own != index)
            def _():
                action(index)

    turned_top = g2[2:4].reshape(2 * cols, 2 * CH).T
    turned_bottom = g2[12:14].reshape(2 * cols, 2 * CH).T
    for a in range(3):
        total = acc[a] + tap_rows(0, a, turned_top) + tap_rows(10, a, turned_bottom)
        parts = (total[CH:, 0:CH], total[0:CH, 0:CH], total[0:CH, CH:])
        for b in range(3):
            value = parts[b].T
            row = (3 * a + b) * CH
            done = 0
            while done < CH:
                block, offset = divmod(row + done, block_rows)
                size = min(CH - done, block_rows - offset)
                taps[block, offset : offset + size] = value[done : done + size].astype(BF16)
                done += size
        others(groups[a], plane, lambda block: plane_copy(block).start())

    def input_rows(m, extra_rows=None):
        product = jnp.dot(
            stacked(g2, m + 2, -d), wi[...], preferred_element_type=F32
        )
        value = folded(product, d, 2)
        own_mask = mref[...].astype(F32)
        value = value + cin[pl.ds(m, 2)].astype(F32)
        if extra_rows is not None:
            value = value + extra_rows
        out_ref[pl.ds(m, 2)] = (value * own_mask).astype(BF16)

    def inner_input(i, carry):
        input_rows(2 + 2 * i)
        return carry

    lax.fori_loop(0, 4, inner_input, 0)

    plane_in[plane] = taps[plane]
    others((0, blocks), plane, lambda source: plane_arrival(source).wait_recv())
    total = plane_in[0].astype(F32)
    for source in range(1, blocks):
        total = total + plane_in[source].astype(F32)
    plane_sum[...] = total

    def column_copy(index):
        return pltpu.make_async_remote_copy(
            src_ref=piece.at[index],
            dst_ref=piece_in.at[column],
            send_sem=z_send.at[index],
            recv_sem=z_recv.at[column],
            device_id=column_device(index),
            device_id_type=MESH,
        )

    def column_arrival(source):
        return pltpu.make_async_remote_copy(
            src_ref=piece.at[source],
            dst_ref=piece_in.at[source],
            send_sem=z_send.at[source],
            recv_sem=z_recv.at[source],
            device_id=column_device(source),
            device_id_type=MESH,
        )

    for index in range(2 * nz):
        start = chip_rows * (index // 2) + (chip_rows - core_rows) * (index % 2)
        piece[index] = plane_sum[start : start + core_rows]
    others((0, 2 * nz), column, lambda index: column_copy(index).start())
    piece_in[column] = piece[column]

    for side in range(2):
        for k in range(2):
            rim_copy(1 - side, k).wait_recv()

    def rim_rows(side, rate, edge):
        got = rim_in[side]
        nothing = jnp.zeros_like(got[0:1])
        wide = rate == 2
        if side == 0:
            rows = jnp.concatenate(
                [jnp.where(wide, got[0:1], got[1:2]), jnp.where(wide, got[1:2], nothing)], axis=0
            )
            weight = wi[4 * CH : 6 * CH]
        else:
            rows = jnp.concatenate(
                [jnp.where(wide, got[0:1], nothing), jnp.where(wide, got[1:2], got[0:1])], axis=0
            )
            weight = wi[0 : 2 * CH]
        rows = jnp.where(edge, jnp.zeros_like(rows), rows)
        gf[:, 0:cols] = rows.astype(F32)
        rim2[:, :, 0:CH] = rows
        rim2[:, :, CH:] = gf[:, pl.ds(rate, cols)].astype(BF16)
        product = jnp.dot(
            rim2[...].reshape(2 * cols, 2 * CH), weight, preferred_element_type=F32
        )
        return folded(product, rate, 2)

    input_rows(0, rim_rows(0, d_up, r == 0))
    input_rows(10, rim_rows(1, d_down, r == tiles_total - 1))

    for side in range(2):
        for k in range(2):
            halo_copy(side, k).wait_send()
            rim_copy(side, k).wait_send()
    others((0, blocks), plane, lambda block: plane_copy(block).wait_send())
    others((0, 2 * nz), column, lambda index: column_copy(index).wait_send())
    others((0, 2 * nz), column, lambda source: column_arrival(source).wait_recv())

    final = piece_in[0]
    for source in range(1, 2 * nz):
        final = final + piece_in[source]
    final = final * (1.0 / math.sqrt(cells))
    if chip_rows % 2 == 0:
        wout_ref[...] = final
    else:
        lane = lax.broadcasted_iota(jnp.int32, (1, CH), 1)
        turned = jnp.concatenate([final[:, CH // 2 :], final[:, : CH // 2]], axis=1)
        for k in range(core_rows):
            upper = turned[k : k + 1]
            if k + 1 < core_rows:
                upper = jnp.where(lane < CH // 2, upper, turned[k + 1 : k + 2])
            value = jnp.where(c == 0, final[k : k + 1], upper).reshape(CH)
            if k + 1 < core_rows:
                wout_ref[k * CH : (k + 1) * CH] = value
            else:
                wout_ref[k * CH :] = value[: CH // 2]


def shards(sizes, features, cotangent, tile_mask, work_lists, dilations, conv_weight, conv_bias):
    ny, nx, nz = sizes
    own_strip = features[0]
    own_cotan = cotangent[0]
    cols = own_strip.shape[1]
    blocks = ny * nx
    block_rows = TAPS * CH // blocks
    chip_rows = block_rows // nz
    cells = blocks * nz * 2 * work_lists.shape[2] * TILE * TILE
    odd = chip_rows % 2
    grad_shape = (chip_rows * CH // 2,) if odd else (chip_rows // 2, CH)
    vmem = pl.BlockSpec(memory_space=pltpu.VMEM)
    hbm = pl.BlockSpec(memory_space=pltpu.HBM)
    dma = pltpu.SemaphoreType.DMA
    operands = (
        dilations,
        tile_mask.reshape(1, -1),
        conv_bias.reshape(1, -1),
        conv_weight,
        own_strip,
        own_cotan,
    )
    input_grad, chip_grad = pl.pallas_call(
        functools.partial(kernel, sizes, cells),
        out_shape=(
            jax.ShapeDtypeStruct(own_strip.shape, BF16),
            jax.ShapeDtypeStruct(grad_shape, F32),
        ),
        in_specs=[hbm] * 6,
        out_specs=(vmem, vmem),
        scratch_shapes=[
            pltpu.SMEM(dilations.shape, jnp.int32),
            pltpu.VMEM((1, cols // TILE), jnp.int32),
            pltpu.VMEM((1, CH), F32),
            pltpu.VMEM(conv_weight.shape, BF16),
            pltpu.VMEM((TILE, cols, CH), BF16),
            pltpu.VMEM((TILE, cols, CH), BF16),
            pltpu.VMEM((cols, CH), BF16),
            pltpu.VMEM((2, HALO, cols, CH), BF16),
            pltpu.VMEM((2, HALO, cols, CH), BF16),
            pltpu.VMEM((2, HALO, cols, CH), BF16),
            pltpu.VMEM((2, HALO, cols, CH), BF16),
            pltpu.VMEM((16, cols + PAD, CH), F32),
            pltpu.VMEM((16, cols, 2 * CH), BF16),
            pltpu.VMEM((2, cols + PAD, CH), F32),
            pltpu.VMEM((16, cols, 2 * CH), BF16),
            pltpu.VMEM((2, cols + PAD, CH), F32),
            pltpu.VMEM((2, cols, 2 * CH), BF16),
            pltpu.VMEM((2, 4, cols, 2 * CH), BF16),
            pltpu.VMEM((2, 2, cols, 2 * CH), F32),
            pltpu.VMEM((6 * CH, 2 * CH), BF16),
            pltpu.VMEM((6 * CH, 2 * CH), BF16),
            pltpu.VMEM((3, 2 * CH, 2 * CH), F32),
            pltpu.VMEM((blocks, block_rows, CH), BF16),
            pltpu.VMEM((blocks, block_rows, CH), BF16),
            pltpu.VMEM((block_rows, CH), F32),
            pltpu.VMEM((2 * nz, (chip_rows + 1) // 2, CH), F32),
            pltpu.VMEM((2 * nz, (chip_rows + 1) // 2, CH), F32),
            dma((6,)),
            dma((2, 2)),
            dma((2, 2)),
            dma((2, 2)),
            dma((2, 2)),
            dma((blocks,)),
            dma((blocks,)),
            dma((2 * nz,)),
            dma((2 * nz,)),
        ],
        compiler_params=pltpu.CompilerParams(
            collective_id=0, has_side_effects=True, vmem_limit_bytes=28 * 1024 * 1024
        ),
    )(*[pltpu.with_memory_space_constraint(value, pltpu.HBM) for value in operands])
    return (input_grad[None], chip_grad.reshape(-1))


def torus_sizes(devices):
    return (4, 4, devices // 16)


def solution(mesh):
    ny, nx, nz = torus_sizes(mesh.shape["tile"])
    torus = Mesh(mesh.devices.reshape(ny, nx, nz, mesh.shape["dp"]), TILE_DP)
    in_specs = (
        P("dp", TILE_AXES, None, None),
        P("dp", TILE_AXES, None, None),
        P("dp", TILE_AXES, None),
        P("dp", None, None),
        P("dp", None),
        P(),
        P(),
    )
    out_specs = (P("dp", TILE_AXES, None, None), P(TILE_DP))
    return jax.shard_map(
        functools.partial(shards, (ny, nx, nz)),
        mesh=torus,
        in_specs=in_specs,
        out_specs=out_specs,
        check_vma=False,
    )
```

time: 37.9 us -> 33.6 us (0.89)
  Pallas kernels: 35.6 us -> 31.3 us
    pallas_call x1, Pallas kernels: 35.6 us -> 31.3 us  [shards(): pl.pallas_call(functools.partial(kernel, sizes, cells), out_shape=(jax.Sh...]
where the time goes in v2:
time: 33.6 us; the launch traced here: 33.5 us
  Pallas kernels  31.3 us (93%)
  local copies, waits for them, and re-layouts  1.61 us (5%)
  between operations  0.64 us (2%)
    pallas_call x1, Pallas kernels, shards(): pl.pallas_call(functools.partial(kernel, sizes, cells), out_shape=(jax.Sh...  31.3 us
    unnamed x2, local copies, waits for them, and re-layouts  1.61 us

profile of v2, /device:TPU:1, one launch (start us, length us, event | category | flops | bytes accessed | tf_op | source)
XLA Modules:
  0.0 33.5 jit_solution(1298734449412173512)
XLA Ops:
  0.6 31.3 %shard_map.77 = (bf16[12,384,128]{2,1,0:T(8,128)(2,1)S(1)}, f32[576]{0:T(1024)S(1)}) custom-call(s32[1,128]{1,0:T(1,128)} %dil_hbm.1, s32[1,32]{1,0:T(1,128)} %bitcast.8, f32[1,128]{1,0:T(1,128)} %bitcast.9, bf16[3,3,128,128]{3,2,1,0:T(8,128)(2,1)} %w_hbm.1, bf16[12,384,128]{2,1,0:T(8,128)(2,1)} %bitcast.6, bf16[12,384,128]{2,1,0:T(8,128)(2,1)} %bitcast.7), custom_call_target="tpu_custom_call" | custom-call | tf_op jit(solution)/shard_map/pallas_call | solution.py:485
  31.9 1.0 %copy.10 = bf16[1,12,384,128]{3,2,1,0:T(8,128)(2,1)} copy(bf16[1,12,384,128]{3,2,1,0:T(8,128)(2,1)S(1)} %bitcast.5) | data formatting | bytes 2359296
  32.9 0.6 %copy.11 = f32[576]{0:T(1024)} copy(f32[576]{0:T(1024)S(1)} %get-tuple-element.9) | data formatting | bytes 4608

commit v3 on v2

--- a/solution.py
+++ b/solution.py
@@ -14,6 +14,7 @@
 CH = 128
 TAPS = 9
 PAD = 8
+CHUNK = 96
 TILE_AXES = ("tile_0", "tile_1", "tile_2")
 TILE_DP = ("tile_0", "tile_1", "tile_2", "dp")
 MESH = pl.DeviceIdType.MESH
@@ -54,7 +55,8 @@
     yf,
     rim2,
     xh,
-    pr,
+    pa,
+    pb,
     wf,
     wi,
     acc,
@@ -63,6 +65,7 @@
     plane_sum,
     piece,
     piece_in,
+    entered,
     load_sem,
     halo_send,
     halo_recv,
@@ -114,23 +117,29 @@
     load_w.start()
     load_c.start()
 
+    def tell(semaphore, device):
+        pl.semaphore_signal(semaphore, inc=1, device_id=device, device_id_type=MESH)
+
+    def along_x(step):
+        return at(y, lax.rem(x + step, nx), z, c)
+
+    def along_y(step):
+        return at(lax.rem(y + step, ny), x, z, c)
+
+    def along_z(step):
+        return at(y, x, lax.rem(z + step, nz), c)
+
+    partner = at(y, x, z, 1 - c)
     barrier = pltpu.get_barrier_semaphore()
-    pl.semaphore_signal(barrier, inc=1, device_id=row_device(r - 1), device_id_type=MESH)
-    pl.semaphore_signal(barrier, inc=1, device_id=row_device(r + 1), device_id_type=MESH)
-    for step in range(1, blocks):
-        pl.semaphore_signal(
-            barrier,
-            inc=1,
-            device_id=plane_device(lax.rem(plane + step, blocks)),
-            device_id_type=MESH,
-        )
-    for step in range(1, 2 * nz):
-        pl.semaphore_signal(
-            barrier,
-            inc=1,
-            device_id=column_device(lax.rem(column + step, 2 * nz)),
-            device_id_type=MESH,
-        )
+    tell(barrier, row_device(r - 1))
+    tell(barrier, row_device(r + 1))
+    for step in range(1, nx):
+        tell(barrier, along_x(step))
+    for step in range(1, ny):
+        tell(barrier, along_y(step))
+    tell(barrier, along_z(1))
+    tell(barrier, along_z(nz - 1))
+    tell(barrier, partner)
 
     col = lax.broadcasted_iota(jnp.int32, (cols, cols // TILE), 0)
     tile = lax.broadcasted_iota(jnp.int32, (cols, cols // TILE), 1) * TILE
@@ -150,43 +159,7 @@
     own = mref[...]
     halo_out[0] = xin[0:2] * own
     halo_out[1] = xin[10:12] * own
-    load_w.wait()
-    zero = jnp.zeros((CH, CH), BF16)
-    for a in range(3):
-        base = 2 * CH * a
-        wf[base : base + CH, 0:CH] = w_ref[a, 1]
-        wf[base : base + CH, CH:] = w_ref[a, 0]
-        wf[base + CH : base + 2 * CH, 0:CH] = w_ref[a, 2]
-        wf[base + CH : base + 2 * CH, CH:] = zero
-        wi[base : base + CH, 0:CH] = w_ref[a, 1].T
-        wi[base : base + CH, CH:] = w_ref[a, 2].T
-        wi[base + CH : base + 2 * CH, 0:CH] = w_ref[a, 0].T
-        wi[base + CH : base + 2 * CH, CH:] = zero
-
-    margin_x = jnp.zeros((xf.shape[0], PAD, CH), F32)
-    xf[:, cols:] = margin_x
-    margin_g = jnp.zeros((2, PAD, CH), F32)
-    gf[:, cols:] = margin_g
-    yf[:, 0:PAD] = margin_g
-    g2[0:2] = jnp.zeros((2, cols, 2 * CH), BF16)
-    g2[14:16] = jnp.zeros((2, cols, 2 * CH), BF16)
-    x2[0:2] = jnp.zeros((2, cols, 2 * CH), BF16)
-    x2[14:16] = jnp.zeros((2, cols, 2 * CH), BF16)
-    xh[0, 2:4] = jnp.zeros((2, cols, 2 * CH), BF16)
-    xh[1, 0:2] = jnp.zeros((2, cols, 2 * CH), BF16)
-
-    def put_x(row, value):
-        xf[pl.ds(row, 2), 0:cols] = value.astype(F32)
-        x2[pl.ds(row, 2), :, 0:CH] = value
-        x2[pl.ds(row, 2), :, CH:] = xf[pl.ds(row, 2), pl.ds(d, cols)].astype(BF16)
-
-    def own_rows(i, carry):
-        put_x(2 + 2 * i, xin[pl.ds(2 * i, 2)] * mref[...])
-        return carry
-
-    lax.fori_loop(0, TILE // 2, own_rows, 0)
-
-    pl.semaphore_wait(barrier, 2 + (blocks - 1) + (2 * nz - 1))
+    pl.semaphore_wait(barrier, 2 + (nx - 1) + (ny - 1) + 2 + 1)
 
     def row_copy(sent, got, send, recv, side, k):
         return pltpu.make_async_remote_copy(
@@ -209,6 +182,57 @@
     halo_copy(0, 1).start()
     halo_copy(1, 0).start()
 
+    for step in range(1, nx):
+        tell(entered.at[0], along_x(step))
+    tell(entered.at[1], along_z(1))
+    tell(entered.at[1], along_z(nz - 1))
+
+    load_w.wait()
+    zero = jnp.zeros((CH, CH), BF16)
+    for a in range(3):
+        base = 2 * CH * a
+        wf[base : base + CH, 0:CH] = w_ref[a, 1]
+        wf[base : base + CH, CH:] = w_ref[a, 0]
+        wf[base + CH : base + 2 * CH, 0:CH] = w_ref[a, 2]
+        wf[base + CH : base + 2 * CH, CH:] = zero
+
+    margin_x = jnp.zeros((xf.shape[0], PAD, CH), F32)
+    xf[:, cols:] = margin_x
+    gf[:, cols:] = jnp.zeros((gf.shape[0], PAD, CH), F32)
+    yf[:, 0:PAD] = jnp.zeros((2, PAD, CH), F32)
+    pb[:, 0:PAD] = jnp.zeros((TILE, PAD, CH), F32)
+    g2[0:2] = jnp.zeros((2, cols, 2 * CH), BF16)
+    g2[14:16] = jnp.zeros((2, cols, 2 * CH), BF16)
+    x2[0:2] = jnp.zeros((2, cols, 2 * CH), BF16)
+    x2[14:16] = jnp.zeros((2, cols, 2 * CH), BF16)
+    xh[0, 2:4] = jnp.zeros((2, cols, 2 * CH), BF16)
+    xh[1, 0:2] = jnp.zeros((2, cols, 2 * CH), BF16)
+
+    chunks = range(0, cols, CHUNK)
+
+    def put_x(row, get, places):
+        for q in chunks:
+            value = get(q)
+            xf[row, q : q + CHUNK] = value.astype(F32)
+            for ref, index in places:
+                ref[(*index, slice(q, q + CHUNK), slice(0, CH))] = value
+
+    def move_x(row, places):
+        for q in chunks:
+            moved = xf[row, pl.ds(d + q, CHUNK)].astype(BF16)
+            for ref, index in places:
+                ref[(*index, slice(q, q + CHUNK), slice(CH, 2 * CH))] = moved
+
+    for row in range(TILE + 1):
+        if row < TILE:
+            put_x(
+                row + 2,
+                lambda q: xin[row, q : q + CHUNK] * mref[q : q + CHUNK],
+                [(x2, (row + 2,))],
+            )
+        if row > 0:
+            move_x(row + 1, [(x2, (row + 1,))])
+
     load_c.wait()
 
     def stacked(ref, row, shift):
@@ -223,64 +247,77 @@
         yf[0:n, PAD:] = product[:, CH:].reshape(n, cols, CH)
         return product[:, 0:CH].reshape(n, cols, CH) + yf[0:n, pl.ds(PAD - shift, cols)]
 
-    def grad_rows(product, p, n):
-        pre = folded(product, d, n) + bias_ref[...]
-        turn = 0.5 * jnp.tanh(0.5 * pre)
-        cot = (cin[pl.ds(p, n)] * mref[...]).astype(F32)
-        grad = (cot * (0.5 + turn) * (1.0 + pre * (0.5 - turn))).astype(BF16)
-        gf[0:n, 0:cols] = grad.astype(F32)
-        g2[pl.ds(p + 2, n), :, 0:CH] = grad
-        g2[pl.ds(p + 2, n), :, CH:] = gf[0:n, pl.ds(d, cols)].astype(BF16)
-        return grad
-
-    def inner_rows(i, carry):
-        p = 2 + 2 * i
+    def forward(p):
         product = jnp.dot(stacked(x2, p + 2, d), wf[...], preferred_element_type=F32)
-        grad_rows(product, p, 2)
-        return carry
-
-    lax.fori_loop(0, 4, inner_rows, 0)
-
-    for side in range(2):
-        product = jnp.dot(
-            stacked(x2, 2 + 10 * side, d), wf[...], preferred_element_type=F32
-        )
-        pr[side] = product.reshape(2, cols, 2 * CH)
-
-    acc[...] = jnp.zeros_like(acc)
-
-    def tap_rows(p, a, turned):
-        shifted = x2[pl.ds(p + 2 + (a - 1) * d, 2)].reshape(2 * cols, 2 * CH)
+        pa[p : p + 2] = product[:, 0:CH].reshape(2, cols, CH)
+        pb[p : p + 2, PAD:] = product[:, CH:].reshape(2, cols, CH)
+
+    def grad_row(p, also=None):
+        for q in chunks:
+            pre = pa[p, q : q + CHUNK] + pb[p, pl.ds(PAD - d + q, CHUNK)] + bias_ref[...]
+            turn = 0.5 * jnp.tanh(0.5 * pre)
+            cot = (cin[p, q : q + CHUNK] * mref[q : q + CHUNK]).astype(F32)
+            grad = (cot * (0.5 + turn) * (1.0 + pre * (0.5 - turn))).astype(BF16)
+            gf[p, q : q + CHUNK] = grad.astype(F32)
+            g2[p + 2, q : q + CHUNK, 0:CH] = grad
+            if also is not None:
+                rim_out[(*also, slice(q, q + CHUNK))] = grad
+        for q in chunks:
+            g2[p + 2, q : q + CHUNK, CH:] = gf[p, pl.ds(d + q, CHUNK)].astype(BF16)
+
+    def tap_rows(p, n, a, turned):
+        shifted = x2[pl.ds(p + 2 + (a - 1) * d, n)].reshape(n * cols, 2 * CH)
         return jnp.dot(turned, shifted, preferred_element_type=F32)
 
-    def inner_taps(i, carry):
-        p = 2 + 2 * i
-        turned = g2[pl.ds(p + 2, 2)].reshape(2 * cols, 2 * CH).T
+    def inner_taps(p):
+        turned = g2[p + 2 : p + 6].reshape(4 * cols, 2 * CH).T
         for a in range(3):
-            acc[a] += tap_rows(p, a, turned)
-        return carry
-
-    lax.fori_loop(0, 4, inner_taps, 0)
+            value = tap_rows(p, 4, a, turned)
+            acc[a] = value if p == 2 else acc[a] + value
+
+    forward(2)
+    forward(4)
+    grad_row(2)
+    grad_row(3)
+    forward(6)
+    grad_row(4)
+    grad_row(5)
+    inner_taps(2)
+    forward(8)
+    grad_row(6)
+    grad_row(7)
+    forward(0)
+    grad_row(8)
+    grad_row(9)
+    forward(10)
+    inner_taps(6)
+
+    pl.semaphore_wait(entered.at[0], nx - 1)
+    pl.semaphore_wait(entered.at[1], 2)
+    if nz > 4:
+        tell(entered.at[2], along_z(2))
+        tell(entered.at[2], along_z(nz - 2))
 
     def put_halo(side, k):
-        got = halo_in[side, k]
         edge = r == (0 if side == 0 else tiles_total - 1)
-        value = jnp.where(edge, jnp.zeros_like(got), got)
         row = 14 * side + k
-        xf[row, 0:cols] = value.astype(F32)
-        moved = xf[row, pl.ds(d, cols)].astype(BF16)
-        x2[row, :, 0:CH] = value
-        x2[row, :, CH:] = moved
-        xh[side, 2 * side + k, :, 0:CH] = value
-        xh[side, 2 * side + k, :, CH:] = moved
+        places = [(x2, (row,)), (xh, (side, 2 * side + k))]
+
+        def get(q):
+            got = halo_in[side, k, q : q + CHUNK]
+            return jnp.where(edge, jnp.zeros_like(got), got)
+
+        put_x(row, get, places)
+        move_x(row, places)
 
     def rim_row(side, k):
         at_row = k + 2 - d if side == 0 else k + d
         weight = wf[4 * CH * side : 4 * CH * side + 2 * CH]
-        product = pr[side, k] + jnp.dot(
-            xh[side, at_row], weight, preferred_element_type=F32
-        )
-        rim_out[side, k] = grad_rows(product, 10 * side + k, 1)[0]
+        product = jnp.dot(xh[side, at_row], weight, preferred_element_type=F32)
+        p = 10 * side + k
+        pa[p] += product[:, 0:CH]
+        pb[p, PAD:] += product[:, CH:]
+        grad_row(p, (side, k))
 
     def halo_wait(side, k):
         halo_copy(1 - side, k).wait_recv()
@@ -302,13 +339,6 @@
     rim_copy(0, 0).start()
     rim_copy(1, 1).start()
 
-    groups = []
-    first = 0
-    for a in range(3):
-        last = (3 * CH * (a + 1)) // block_rows
-        groups.append((first, last))
-        first = last
-
     def plane_copy(block):
         return pltpu.make_async_remote_copy(
             src_ref=taps.at[block],
@@ -329,17 +359,10 @@
             device_id_type=MESH,
         )
 
-    def others(count, own, action):
-        for index in range(count[0], count[1]):
-
-            @pl.when(own != index)
-            def _():
-                action(index)
-
     turned_top = g2[2:4].reshape(2 * cols, 2 * CH).T
     turned_bottom = g2[12:14].reshape(2 * cols, 2 * CH).T
     for a in range(3):
-        total = acc[a] + tap_rows(0, a, turned_top) + tap_rows(10, a, turned_bottom)
+        total = acc[a] + tap_rows(0, 2, a, turned_top) + tap_rows(10, 2, a, turned_bottom)
         parts = (total[CH:, 0:CH], total[0:CH, 0:CH], total[0:CH, CH:])
         for b in range(3):
             value = parts[b].T
@@ -350,7 +373,24 @@
                 size = min(CH - done, block_rows - offset)
                 taps[block, offset : offset + size] = value[done : done + size].astype(BF16)
                 done += size
-        others(groups[a], plane, lambda block: plane_copy(block).start())
+        ready = range(3 * CH * a // block_rows, 3 * CH * (a + 1) // block_rows)
+        for block in ready:
+
+            @pl.when(plane != block)
+            def _():
+                plane_copy(block).start()
+
+
+    for a in range(3):
+        base = 2 * CH * a
+        wi[base : base + CH, 0:CH] = w_ref[a, 1].T
+        wi[base : base + CH, CH:] = w_ref[a, 2].T
+        wi[base + CH : base + 2 * CH, 0:CH] = w_ref[a, 0].T
+        wi[base + CH : base + 2 * CH, CH:] = zero
+
+    if nz > 4:
+        pl.semaphore_wait(entered.at[2], 2)
+    tell(entered.at[3], partner)
 
     def input_rows(m, extra_rows=None):
         product = jnp.dot(
@@ -370,7 +410,8 @@
     lax.fori_loop(0, 4, inner_input, 0)
 
     plane_in[plane] = taps[plane]
-    others((0, blocks), plane, lambda source: plane_arrival(source).wait_recv())
+    for step in range(1, blocks):
+        plane_arrival(lax.rem(plane + step, blocks)).wait_recv()
     total = plane_in[0].astype(F32)
     for source in range(1, blocks):
         total = total + plane_in[source].astype(F32)
@@ -399,7 +440,10 @@
     for index in range(2 * nz):
         start = chip_rows * (index // 2) + (chip_rows - core_rows) * (index % 2)
         piece[index] = plane_sum[start : start + core_rows]
-    others((0, 2 * nz), column, lambda index: column_copy(index).start())
+    pl.semaphore_wait(entered.at[3], 1)
+    steps = range(1, 2 * nz)
+    for step in steps:
+        column_copy(lax.rem(column + step, 2 * nz)).start()
     piece_in[column] = piece[column]
 
     for side in range(2):
@@ -421,9 +465,9 @@
             )
             weight = wi[0 : 2 * CH]
         rows = jnp.where(edge, jnp.zeros_like(rows), rows)
-        gf[:, 0:cols] = rows.astype(F32)
+        gf[0:2, 0:cols] = rows.astype(F32)
         rim2[:, :, 0:CH] = rows
-        rim2[:, :, CH:] = gf[:, pl.ds(rate, cols)].astype(BF16)
+        rim2[:, :, CH:] = gf[0:2, pl.ds(rate, cols)].astype(BF16)
         product = jnp.dot(
             rim2[...].reshape(2 * cols, 2 * CH), weight, preferred_element_type=F32
         )
@@ -436,9 +480,12 @@
         for k in range(2):
             halo_copy(side, k).wait_send()
             rim_copy(side, k).wait_send()
-    others((0, blocks), plane, lambda block: plane_copy(block).wait_send())
-    others((0, 2 * nz), column, lambda index: column_copy(index).wait_send())
-    others((0, 2 * nz), column, lambda source: column_arrival(source).wait_recv())
+    for step in range(1, blocks):
+        plane_copy(lax.rem(plane + step, blocks)).wait_send()
+    for step in steps:
+        column_copy(lax.rem(column + step, 2 * nz)).wait_send()
+    for step in steps:
+        column_arrival(lax.rem(column + step, 2 * nz)).wait_recv()
 
     final = piece_in[0]
     for source in range(1, 2 * nz):
@@ -504,12 +551,13 @@
             pltpu.VMEM((2, HALO, cols, CH), BF16),
             pltpu.VMEM((16, cols + PAD, CH), F32),
             pltpu.VMEM((16, cols, 2 * CH), BF16),
-            pltpu.VMEM((2, cols + PAD, CH), F32),
+            pltpu.VMEM((TILE, cols + PAD, CH), F32),
             pltpu.VMEM((16, cols, 2 * CH), BF16),
             pltpu.VMEM((2, cols + PAD, CH), F32),
             pltpu.VMEM((2, cols, 2 * CH), BF16),
             pltpu.VMEM((2, 4, cols, 2 * CH), BF16),
-            pltpu.VMEM((2, 2, cols, 2 * CH), F32),
+            pltpu.VMEM((TILE, cols, CH), F32),
+            pltpu.VMEM((TILE, cols + PAD, CH), F32),
             pltpu.VMEM((6 * CH, 2 * CH), BF16),
             pltpu.VMEM((6 * CH, 2 * CH), BF16),
             pltpu.VMEM((3, 2 * CH, 2 * CH), F32),
@@ -518,6 +566,7 @@
             pltpu.VMEM((block_rows, CH), F32),
             pltpu.VMEM((2 * nz, (chip_rows + 1) // 2, CH), F32),
             pltpu.VMEM((2 * nz, (chip_rows + 1) // 2, CH), F32),
+            pltpu.SemaphoreType.REGULAR((4,)),
             dma((6,)),
             dma((2, 2)),
             dma((2, 2)),
@@ -529,7 +578,7 @@
             dma((2 * nz,)),
         ],
         compiler_params=pltpu.CompilerParams(
-            collective_id=0, has_side_effects=True, vmem_limit_bytes=28 * 1024 * 1024
+            collective_id=0, has_side_effects=True, vmem_limit_bytes=40 * 1024 * 1024
         ),
     )(*[pltpu.with_memory_space_constraint(value, pltpu.HBM) for value in operands])
     return (input_grad[None], chip_grad.reshape(-1))

time: 33.6 us -> 32.5 us (0.967)
  Pallas kernels: 31.3 us -> 30.1 us
    pallas_call x1, Pallas kernels: 31.3 us -> 30.1 us  [shards(): pl.pallas_call(functools.partial(kernel, sizes, cells), out_shape=(jax.Sh...]
where the time goes in v3:
time: 32.5 us; the launch traced here: 32.3 us
  Pallas kernels  30.1 us (93%)
  local copies, waits for them, and re-layouts  1.61 us (5%)
  between operations  0.64 us (2%)
    pallas_call x1, Pallas kernels, shards(): pl.pallas_call(functools.partial(kernel, sizes, cells), out_shape=(jax.Sh...  30.1 us
    unnamed x2, local copies, waits for them, and re-layouts  1.61 us

profile of v3, /device:TPU:1, one launch (start us, length us, event | category | flops | bytes accessed | tf_op | source)
XLA Modules:
  0.0 32.3 jit_solution(755897260871001568)
XLA Ops:
  0.6 30.1 %shard_map.77 = (bf16[12,384,128]{2,1,0:T(8,128)(2,1)S(1)}, f32[576]{0:T(1024)S(1)}) custom-call(s32[1,128]{1,0:T(1,128)} %dil_hbm.1, s32[1,32]{1,0:T(1,128)} %bitcast.8, f32[1,128]{1,0:T(1,128)} %bitcast.9, bf16[3,3,128,128]{3,2,1,0:T(8,128)(2,1)} %w_hbm.1, bf16[12,384,128]{2,1,0:T(8,128)(2,1)} %bitcast.6, bf16[12,384,128]{2,1,0:T(8,128)(2,1)} %bitcast.7), custom_call_target="tpu_custom_call" | custom-call | tf_op jit(solution)/shard_map/pallas_call | solution.py:532
  30.7 1.0 %copy.10 = bf16[1,12,384,128]{3,2,1,0:T(8,128)(2,1)} copy(bf16[1,12,384,128]{3,2,1,0:T(8,128)(2,1)S(1)} %bitcast.5) | data formatting | bytes 2359296
  31.7 0.6 %copy.11 = f32[576]{0:T(1024)} copy(f32[576]{0:T(1024)S(1)} %get-tuple-element.9) | data formatting | bytes 4608

commit v4 on v3

--- a/solution.py
+++ b/solution.py
@@ -505,6 +505,19 @@
                 wout_ref[k * CH : (k + 1) * CH] = value
             else:
                 wout_ref[k * CH :] = value[: CH // 2]
+
+
+def place(grad_ref, taps_ref, grad_hbm, taps_hbm, sem):
+    copies = [pltpu.make_async_copy(taps_ref, taps_hbm, sem.at[0])]
+    for k in range(4):
+        rows = pl.ds(3 * k, 3)
+        copies.append(
+            pltpu.make_async_copy(grad_ref.at[rows], grad_hbm.at[rows], sem.at[k + 1])
+        )
+    for copy in copies:
+        copy.start()
+    for copy in copies:
+        copy.wait()
 
 
 def shards(sizes, features, cotangent, tile_mask, work_lists, dilations, conv_weight, conv_bias):
@@ -581,6 +594,17 @@
             collective_id=0, has_side_effects=True, vmem_limit_bytes=40 * 1024 * 1024
         ),
     )(*[pltpu.with_memory_space_constraint(value, pltpu.HBM) for value in operands])
+    input_grad, chip_grad = pl.pallas_call(
+        place,
+        out_shape=(
+            jax.ShapeDtypeStruct(input_grad.shape, BF16),
+            jax.ShapeDtypeStruct(chip_grad.shape, F32),
+        ),
+        in_specs=[vmem, vmem],
+        out_specs=(hbm, hbm),
+        scratch_shapes=[dma((5,))],
+        compiler_params=pltpu.CompilerParams(vmem_limit_bytes=4 * 1024 * 1024),
+    )(input_grad, chip_grad)
     return (input_grad[None], chip_grad.reshape(-1))
 
 

time: 32.5 us -> 32 us (0.985)
  local copies, waits for them, and re-layouts: 1.61 us -> 0 us
  Pallas kernels: 30.1 us -> 31.1 us
    unnamed x2 -> x0, local copies, waits for them, and re-layouts: 1.61 us -> none
    pallas_call x0 -> x1, Pallas kernels: none -> 1.05 us  [shards(): pl.pallas_call(place, out_shape=(jax.ShapeDtypeStruct(input_grad.shape, B...]
where the time goes in v4:
time: 32 us; the launch traced here: 31.7 us
  Pallas kernels  31.1 us (97%)
  between operations  0.64 us (2%)
    pallas_call x1, Pallas kernels, shards(): pl.pallas_call(functools.partial(kernel, sizes, cells), out_shape=(jax.Sh...  30.1 us
    pallas_call x1, Pallas kernels, shards(): pl.pallas_call(place, out_shape=(jax.ShapeDtypeStruct(input_grad.shape, B...  1.05 us

profile of v4, /device:TPU:1, one launch (start us, length us, event | category | flops | bytes accessed | tf_op | source)
XLA Modules:
  0.0 31.7 jit_solution(10636407377199313714)
XLA Ops:
  0.6 30.1 %shard_map.77 = (bf16[12,384,128]{2,1,0:T(8,128)(2,1)S(1)}, f32[576]{0:T(1024)S(1)}) custom-call(s32[1,128]{1,0:T(1,128)} %dil_hbm.1, s32[1,32]{1,0:T(1,128)} %bitcast.7, f32[1,128]{1,0:T(1,128)} %bitcast.8, bf16[3,3,128,128]{3,2,1,0:T(8,128)(2,1)} %w_hbm.1, bf16[12,384,128]{2,1,0:T(8,128)(2,1)} %bitcast.5, bf16[12,384,128]{2,1,0:T(8,128)(2,1)} %bitcast.6), custom_call_target="tpu_custom_call" | custom-call | tf_op jit(solution)/shard_map/pallas_call | solution.py:545
  30.7 1.1 %shard_map.78 = (bf16[12,384,128]{2,1,0:T(8,128)(2,1)}, f32[576]{0:T(1024)}) custom-call(bf16[12,384,128]{2,1,0:T(8,128)(2,1)S(1)} %get-tuple-element.6.grad_ref, f32[576]{0:T(1024)S(1)} %get-tuple-element.7.taps_ref), custom_call_target="tpu_custom_call" | custom-call | tf_op jit(solution)/shard_map/pallas_call | solution.py:597

commit v5 on v4

--- a/solution.py
+++ b/solution.py
@@ -330,6 +330,14 @@
     rim_row(1, 0)
     rim_copy(0, 1).start()
     rim_copy(1, 0).start()
+
+    def turned_row(p):
+        return g2[p + 2].T
+
+    early = (turned_row(1), turned_row(10))
+    for a in range(3):
+        acc[a] += tap_rows(1, 1, a, early[0]) + tap_rows(10, 1, a, early[1])
+
     halo_wait(0, 0)
     halo_wait(1, 1)
     put_halo(0, 0)
@@ -359,10 +367,10 @@
             device_id_type=MESH,
         )
 
-    turned_top = g2[2:4].reshape(2 * cols, 2 * CH).T
-    turned_bottom = g2[12:14].reshape(2 * cols, 2 * CH).T
+    turned_top = turned_row(0)
+    turned_bottom = turned_row(11)
     for a in range(3):
-        total = acc[a] + tap_rows(0, 2, a, turned_top) + tap_rows(10, 2, a, turned_bottom)
+        total = acc[a] + tap_rows(0, 1, a, turned_top) + tap_rows(11, 1, a, turned_bottom)
         parts = (total[CH:, 0:CH], total[0:CH, 0:CH], total[0:CH, CH:])
         for b in range(3):
             value = parts[b].T

time: 32 us -> 32.3 us (level)
  Pallas kernels: 31.1 us -> 31.5 us
    pallas_call x1, Pallas kernels: 30.1 us -> 30.5 us  [shards(): pl.pallas_call(functools.partial(kernel, sizes, cells), out_shape=(jax.Sh...]
where the time goes in v5:
time: 32.3 us; the launch traced here: 32.1 us
  Pallas kernels  31.5 us (98%)
  between operations  0.64 us (2%)
    pallas_call x1, Pallas kernels, shards(): pl.pallas_call(functools.partial(kernel, sizes, cells), out_shape=(jax.Sh...  30.5 us
    pallas_call x1, Pallas kernels, shards(): pl.pallas_call(place, out_shape=(jax.ShapeDtypeStruct(input_grad.shape, B...  1.05 us

profile of v5, /device:TPU:1, one launch (start us, length us, event | category | flops | bytes accessed | tf_op | source)
XLA Modules:
  0.0 32.1 jit_solution(3535137108361368380)
XLA Ops:
  0.6 30.5 %shard_map.77 = (bf16[12,384,128]{2,1,0:T(8,128)(2,1)S(1)}, f32[576]{0:T(1024)S(1)}) custom-call(s32[1,128]{1,0:T(1,128)} %dil_hbm.1, s32[1,32]{1,0:T(1,128)} %bitcast.7, f32[1,128]{1,0:T(1,128)} %bitcast.8, bf16[3,3,128,128]{3,2,1,0:T(8,128)(2,1)} %w_hbm.1, bf16[12,384,128]{2,1,0:T(8,128)(2,1)} %bitcast.5, bf16[12,384,128]{2,1,0:T(8,128)(2,1)} %bitcast.6), custom_call_target="tpu_custom_call" | custom-call | tf_op jit(solution)/shard_map/pallas_call | solution.py:553
  31.1 1.1 %shard_map.78 = (bf16[12,384,128]{2,1,0:T(8,128)(2,1)}, f32[576]{0:T(1024)}) custom-call(bf16[12,384,128]{2,1,0:T(8,128)(2,1)S(1)} %get-tuple-element.6.grad_ref, f32[576]{0:T(1024)S(1)} %get-tuple-element.7.taps_ref), custom_call_target="tpu_custom_call" | custom-call | tf_op jit(solution)/shard_map/pallas_call | solution.py:605
